TPU v7x, 256 devices: a whole 4x4x8 slice. The times are simulated.
256 devices in a mesh: sub: 64 (over x, z, core), col: 4 (over y).
Axes of the slice: x: 4, y: 4, z: 8, core: 2. Of those that a mesh axis runs over, the one named last changes fastest.
Arguments:
- flexibility: bfloat16 [64, 768, 768], P('sub')
- omega: bfloat16 [256, 24576], P('col', 'sub'), may hold values from -6 to 6
- block_row: int32 [64, 6], replicated, may hold values from 0 to 191, as said below
- block_sign: int32 [64, 6], replicated, may hold values from -1 to 1, as said below
Outputs:
- sketch: float32 [256, 24576], P('col', 'sub')
- basis: float32 [256, 24576], P('col', 'sub')
- factor: float32 [256, 256], replicated
Inputs may be any that keep to these rules, and one draw needn't show every extreme that they name: `block_row`: each row block is named by exactly two entries, one whose block_sign is 1 and one whose block_sign is -1. Row block b lies in the sketch columns of sub index b // 3. For any two sub indices p and q, the blocks of p's one substructure name row blocks of q either exactly 2 times or never. `block_sign`: every entry is -1 or 1.
All inputs are finite; a program needn't handle non-finite values.
Results may differ from a plain program's by a relative error of at most 0.0003.
Values may be sent and summed in bfloat16 or wider, within the bound.
A program may use at most 64 MiB of HBM per device.

v0:
```python
import jax
import jax.numpy as jnp
from jax import lax
from jax.sharding import PartitionSpec as P


def rank_within(owners):
    count = owners.shape[-1]
    same = owners[..., :, None] == owners[..., None, :]
    index = jnp.arange(count)
    earlier = index[None, :] < index[:, None]
    return jnp.sum(same & earlier, axis=-1)


def upper_factor(gram):
    order = gram.shape[0]
    index = jnp.arange(order)

    def eliminate(column, state):
        remain, upper = state
        row = lax.dynamic_index_in_dim(remain, column, 0, keepdims=False)
        pivot = jnp.sqrt(lax.dynamic_index_in_dim(row, column, 0, keepdims=False))
        scaled = jnp.where(index >= column, row / pivot, jnp.zeros_like(row))
        upper = lax.dynamic_update_slice_in_dim(upper, scaled[None, :], column, 0)
        remain = remain - scaled[:, None] * scaled[None, :]
        return (remain, upper)

    start = (gram, jnp.zeros_like(gram))
    ignored, upper = lax.fori_loop(0, order, eliminate, start)
    return upper


def upper_inverse(upper):
    order = upper.shape[0]
    index = jnp.arange(order)

    def substitute(turn, inverse):
        column = order - 1 - turn
        row = lax.dynamic_index_in_dim(upper, column, 0, keepdims=False)
        pivot = lax.dynamic_index_in_dim(row, column, 0, keepdims=False)
        unit = (index == column).astype(jnp.float32)
        known = jnp.dot(row, inverse, precision=lax.Precision.HIGHEST)
        solved = (unit - known) / pivot
        return lax.dynamic_update_slice_in_dim(inverse, solved[None, :], column, 0)

    return lax.fori_loop(0, order, substitute, jnp.zeros_like(upper))


def shards(flexibility, omega, block_row, block_sign):
    sub_count = lax.axis_size("sub")
    position = lax.axis_index("sub")
    sub_local = flexibility.shape[0]
    local_dofs = flexibility.shape[1]
    local_blocks = block_row.shape[1]
    block_len = local_dofs // local_blocks
    col_width = omega.shape[0]
    row_count = omega.shape[1]
    owned_blocks = row_count // block_len
    ref_count = sub_local * local_blocks
    capacity = max(2, (ref_count + sub_count - 1) // sub_count)
    slot_count = sub_count * capacity
    all_owner = block_row // owned_blocks
    all_rank = rank_within(all_owner)
    my_signs = lax.dynamic_index_in_dim(block_sign, position, 0, keepdims=False)
    my_slot = lax.dynamic_index_in_dim(all_owner * capacity + all_rank, position, 0, keepdims=False)
    hits = (all_owner == position)[:, None, :] & (
        all_rank[:, None, :] == jnp.arange(capacity)[None, :, None]
    )
    served = jnp.any(hits, axis=-1).reshape(slot_count)
    source_block = jnp.sum(
        jnp.where(hits, (block_row % owned_blocks)[:, None, :], 0), axis=-1
    ).reshape(slot_count)
    blocks = omega.reshape(col_width, owned_blocks, block_len)
    outgoing = jnp.take(blocks, source_block, axis=1).reshape(
        col_width, sub_count, capacity * block_len
    )
    incoming = lax.all_to_all(outgoing, "sub", split_axis=1, concat_axis=1, tiled=True)
    pieces = jnp.take(incoming.reshape(col_width, slot_count, block_len), my_slot, axis=1)
    signed = pieces * my_signs.astype(jnp.bfloat16)[None, :, None]
    response = jnp.einsum(
        "ksj,sij->ksi",
        signed.reshape(col_width, sub_local, local_dofs),
        flexibility,
        preferred_element_type=jnp.float32,
    )
    contrib = response.reshape(col_width, ref_count, block_len)
    route = (my_slot[:, None] == jnp.arange(slot_count)[None, :]).astype(
        jnp.float32
    ) * my_signs.astype(jnp.float32)[:, None]
    outgoing_back = jnp.einsum("krb,rq->kqb", contrib, route, precision=lax.Precision.HIGHEST)
    outgoing_back = outgoing_back.reshape(col_width, sub_count, capacity * block_len)
    returned = lax.all_to_all(outgoing_back, "sub", split_axis=1, concat_axis=1, tiled=True)
    collect = (
        (source_block[:, None] == jnp.arange(owned_blocks)[None, :]) & served[:, None]
    ).astype(jnp.float32)
    sketch = jnp.einsum(
        "kqb,qi->kib",
        returned.reshape(col_width, slot_count, block_len),
        collect,
        precision=lax.Precision.HIGHEST,
    )
    sketch = sketch.reshape(col_width, row_count)
    full = lax.all_gather(sketch, "col", axis=0, tiled=True)
    rows_total = row_count * sub_count
    local_gram = (
        lax.dot_general(full, full, (((1,), (1,)), ((), ())), precision=lax.Precision.HIGHEST)
        / rows_total
    )
    gram = lax.psum(local_gram, "sub")
    upper = upper_factor(gram)
    inverse = upper_inverse(upper)
    column_part = lax.dynamic_slice_in_dim(inverse, lax.axis_index("col") * col_width, col_width, 1)
    basis = lax.dot_general(
        column_part, full, (((0,), (0,)), ((), ())), precision=lax.Precision.HIGHEST
    )
    return (sketch, basis, upper)


def solution(mesh):
    placed = (P("sub", None, None), P("col", "sub"), P(), P())
    return jax.shard_map(
        shards,
        mesh=mesh,
        in_specs=placed,
        out_specs=(P("col", "sub"), P("col", "sub"), P()),
        check_vma=False,
    )
```

profile of v0, /device:TPU:1, one launch (start us, length us, event | category | flops | bytes accessed | tf_op | source)
XLA Modules:
  0.0 1963.2 jit_solution(2266155646979882207)
XLA Ops:
  10.8 2.7 copy.60
  13.6 2.7 gather.11
  16.7 2.5 copy.61
  19.3 13.1 all-to-all-start
  33.0 50.6 %all-to-all-done = bf16[64,64,256]{2,0,1:T(8,128)(2,1)S(1)} async-done(((bf16[64,64,256]{2,0,1:T(8,128)(2,1)}), bf16[64,64,256]{2,0,1:T(8,128)(2,1)S(1)}, u32[]{:S(2)}, u32[]{:S(2)}) %all-to-all-start) | async-done | bytes 2097184 | tf_op jit(solution)/shard_map/all_to_all | solution.py:77
  83.6 2.5 copy.62
  86.2 2.7 reshape.238
  88.8 2.7 copy.63
  91.5 2.2 gather_fusion.1
  94.3 5.2 convolution_bitcast_fusion
  99.5 5.2 reshape.241
  104.7 6.6 copy.65
  111.3 6.0 all-to-all-start.1
  118.0 95.2 %all-to-all-done.1 = f32[64,64,256]{2,0,1:T(8,128)} async-done(((f32[64,64,256]{2,0,1:T(8,128)}), f32[64,64,256]{2,0,1:T(8,128)}, u32[]{:S(2)}, u32[]{:S(2)}) %all-to-all-start.1) | async-done | bytes 4194336 | tf_op jit(solution)/shard_map/all_to_all | solution.py:92
  213.2 6.6 copy.66
  219.8 4.7 reshape.242
  224.5 3.6 fusion.30
  228.1 10.8 all_gather.3
  240.3 174.1 %all-reduce.2.cloned.1.call-done = f32[256,256]{1,0:T(8,128)} async-done(((f32[256,256]{1,0:T(8,128)}), f32[256,256]{1,0:T(8,128)}) %all-reduce.2.cloned.1.call-update) | async-done | bytes 262160 | tf_op jit(solution)/shard_map/psum | solution.py:109
  414.4 1146.5 %while.36 = (s32[]{:T(128)}, f32[256,256]{1,0:T(8,128)}, f32[256,256]{1,0:T(8,128)S(1)}, s32[]{:T(128)}, s32[]{:T(128)}, /*index=5*/s32[]{:T(128)}) while((s32[]{:T(128)}, f32[256,256]{1,0:T(8,128)}, f32[256,256]{1,0:T(8,128)S(1)}, s32[]{:T(128)}, s32[]{:T(128)}, /*index=5*/s32[]{:T(128)}) %tuple.87), condition=%wide.region_5.6_spmd.clone, body=%wide.region_4.5_spmd.clone.sunk | while | flops 132355 | bytes 534141 | solution.py:29
  421.6 1.7 multiply_subtract_fusion.2
  439.5 1.7 multiply_subtract_fusion.2
  466.4 1.7 multiply_subtract_fusion.2
  488.8 1.7 multiply_subtract_fusion.2
  533.5 1.7 multiply_subtract_fusion.2
  542.5 1.7 multiply_subtract_fusion.2
  551.5 1.7 multiply_subtract_fusion.2
  587.2 1.7 multiply_subtract_fusion.2
  681.3 1.7 multiply_subtract_fusion.2
  690.3 1.7 multiply_subtract_fusion.2
  699.2 1.7 multiply_subtract_fusion.2
  748.5 1.7 multiply_subtract_fusion.2
  784.3 1.7 multiply_subtract_fusion.2
  811.2 1.7 multiply_subtract_fusion.2
  847.0 1.7 multiply_subtract_fusion.2
  963.5 1.7 multiply_subtract_fusion.2
  999.3 1.7 multiply_subtract_fusion.2
  1017.2 1.7 multiply_subtract_fusion.2
  1075.5 1.7 multiply_subtract_fusion.2
  1080.0 1.7 multiply_subtract_fusion.2
  1084.5 1.7 multiply_subtract_fusion.2
  1097.9 1.7 multiply_subtract_fusion.2
  1156.1 1.7 multiply_subtract_fusion.2
  1178.5 1.7 multiply_subtract_fusion.2
  1196.4 1.7 multiply_subtract_fusion.2
  1236.7 1.7 multiply_subtract_fusion.2
  1245.7 1.7 multiply_subtract_fusion.2
  1561.0 394.2 %while.37 = (s32[]{:T(128)}, f32[256,256]{1,0:T(8,128)S(1)}, f32[256,256]{1,0:T(8,128)S(1)}, s32[]{:T(128)}, s32[]{:T(128)}, /*index=5*/s32[]{:T(128)}, s32[]{:T(128)}) while((s32[]{:T(128)}, f32[256,256]{1,0:T(8,128)S(1)}, f32[256,256]{1,0:T(8,128)S(1)}, s32[]{:T(128)}, s32[]{:T(128)}, /*index=5*/s32[]{:T(128)}, s32[]{:T(128)}) %tuple.90), condition=%wide.region_7.8_spmd.clone, body=%wide.region_6.7_spmd.clone.sunk | while | flops 787463 | bytes 268455 | solution.py:46
  (2577 shorter events, 1309.0 us)
Async XLA Ops:
  7.2 86.5 %copy-start = (bf16[1,768,768]{2,1,0:T(8,128)(2,1)S(1)}, bf16[1,768,768]{2,1,0:T(8,128)(2,1)}, u32[]{:S(2)}) copy-start(bf16[1,768,768]{2,1,0:T(8,128)(2,1)} %param.8) | copy-start | bytes 3538948
  19.3 13.1 copy-start.3
  19.3 64.4 %all-to-all-start = ((bf16[64,64,256]{2,0,1:T(8,128)(2,1)}), bf16[64,64,256]{2,0,1:T(8,128)(2,1)S(1)}, u32[]{:S(2)}, u32[]{:S(2)}) async-start(bf16[64,64,256]{2,0,1:T(8,128)(2,1)} %copy.61), calls=%async_computation | async-start | bytes 4194304 | tf_op jit(solution)/shard_map/all_to_all | solution.py:77
  111.3 101.9 %all-to-all-start.1 = ((f32[64,64,256]{2,0,1:T(8,128)}), f32[64,64,256]{2,0,1:T(8,128)}, u32[]{:S(2)}, u32[]{:S(2)}) async-start(f32[64,64,256]{2,0,1:T(8,128)} %copy.65), calls=%async_computation.1 | async-start | bytes 8388608 | tf_op jit(solution)/shard_map/all_to_all | solution.py:92
  117.3 297.1 %all-reduce.2.cloned.1.call-start = ((), (), s32[]{:S(2)}) async-start(), calls=%async_computation.2 | async-start | bytes 524288 | tf_op jit(solution)/shard_map/psum | solution.py:109
  228.1 186.3 %copy-start.1 = (f32[8,8,3,128]{3,1,2,0:T(8,128)}, f32[8,8,3,128]{3,1,2,0:T(8,128)S(1)}, u32[]{:S(2)}) copy-start(f32[8,8,3,128]{3,1,2,0:T(8,128)S(1)} %copy.79) | copy-start | bytes 294916
  1955.2 1.1 copy-start.2
Sparse Core Ops, SparseCore 0:
  240.4 173.8 all-reduce.1
where the time goes:
time: 2000 us; the launch traced here: 1960 us
  other arithmetic  800 us (40%)
  local copies, waits for them, and re-layouts  547 us (27%)
  waiting for transfers between devices  320 us (16%)
  loops' own time  193 us (10%)
  matrix products  59.1 us (3%)
    sub x256, other arithmetic, eliminate(): remain = remain - scaled[:, None] * scaled[None, :]  447 us
    dynamic_slice x256, local copies, waits for them, and re-layouts, eliminate(): pivot = jnp.sqrt(lax.dynamic_index_in_dim(row, column, 0, keepdims=False))  325 us
    another operation x1, loops' own time, upper_factor(): ignored, upper = lax.fori_loop(0, order, eliminate, start)  184 us
    select_n x512, other arithmetic, eliminate(): scaled = jnp.where(index >= column, row / pivot, jnp.zeros_like(row))  183 us
    psum x1, waiting for transfers between devices, shards(): gram = lax.psum(local_gram, 'sub')  174 us
    div x256, other arithmetic, substitute(): solved = (unit - known) / pivot  166 us
    dynamic_slice x256, local copies, waits for them, and re-layouts, substitute(): pivot = lax.dynamic_index_in_dim(row, column, 0, keepdims=False)  161 us
    all_to_all x1, waiting for transfers between devices, shards(): lax.all_to_all(outgoing_back, 'sub', split_axis=1, concat_axis=1, tiled=T...  95.2 us
  transfers between devices with their start and end apart: 3, of which 3 were waited for; matrix products, arithmetic and copies ran while one was open for 0% of the time, Pallas kernels for 0%

commit v1 on v0

--- a/solution.py
+++ b/solution.py
@@ -106,7 +106,7 @@
         lax.dot_general(full, full, (((1,), (1,)), ((), ())), precision=lax.Precision.HIGHEST)
         / rows_total
     )
-    gram = lax.psum(local_gram, "sub")
+    gram = jnp.sum(lax.all_gather(local_gram, "sub"), axis=0)
     upper = upper_factor(gram)
     inverse = upper_inverse(upper)
     column_part = lax.dynamic_slice_in_dim(inverse, lax.axis_index("col") * col_width, col_width, 1)

time: 2000 us -> 1150 us (0.57); the launches traced: 1960 us -> 1140 us
  other arithmetic: 800 us -> 210 us
  local copies, waits for them, and re-layouts: 547 us -> 378 us
  waiting for transfers between devices: 320 us -> 244 us
    sub x256, other arithmetic: 447 us -> 28.7 us  [eliminate(): remain = remain - scaled[:, None] * scaled[None, :]]
    select_n x512, other arithmetic: 183 us -> 4.72 us  [eliminate(): scaled = jnp.where(index >= column, row / pivot, jnp.zeros_like(row))]
    psum x1 -> x0, waiting for transfers between devices: 174 us -> none  [shards(): gram = lax.psum(local_gram, 'sub')]
    dynamic_slice x256, local copies, waits for them, and re-layouts: 325 us -> 151 us  [eliminate(): pivot = jnp.sqrt(lax.dynamic_index_in_dim(row, column, 0, keepdims=False))]
    all_gather x0 -> x1, waiting for transfers between devices: none -> 98.6 us  [shards(): gram = jnp.sum(lax.all_gather(local_gram, 'sub'), axis=0)]
where the time goes in v1:
time: 1150 us; the launch traced here: 1140 us
  local copies, waits for them, and re-layouts  378 us (33%)
  waiting for transfers between devices  244 us (21%)
  other arithmetic  210 us (18%)
  loops' own time  200 us (17%)
  matrix products  59.1 us (5%)
  starting transfers between devices  19.4 us (2%)
  between operations  14.3 us (1%)
    another operation x1, loops' own time, upper_factor(): ignored, upper = lax.fori_loop(0, order, eliminate, start)  191 us
    div x256, other arithmetic, substitute(): solved = (unit - known) / pivot  166 us
    dynamic_slice x256, local copies, waits for them, and re-layouts, substitute(): pivot = lax.dynamic_index_in_dim(row, column, 0, keepdims=False)  161 us
    dynamic_slice x256, local copies, waits for them, and re-layouts, eliminate(): pivot = jnp.sqrt(lax.dynamic_index_in_dim(row, column, 0, keepdims=False))  151 us
    all_gather x1, waiting for transfers between devices, shards(): gram = jnp.sum(lax.all_gather(local_gram, 'sub'), axis=0)  98.6 us
    all_to_all x1, waiting for transfers between devices, shards(): lax.all_to_all(outgoing_back, 'sub', split_axis=1, concat_axis=1, tiled=T...  95.2 us
    all_to_all x1, waiting for transfers between devices, shards(): lax.all_to_all(outgoing, 'sub', split_axis=1, concat_axis=1, tiled=True)  50.6 us
    dot_general x256, matrix products, substitute(): known = jnp.dot(row, inverse, precision=lax.Precision.HIGHEST)  47.3 us
  transfers between devices with their start and end apart: 3, of which 3 were waited for; matrix products, arithmetic and copies ran while one was open for 0% of the time, Pallas kernels for 0%

profile of v1, /device:TPU:1, one launch (start us, length us, event | category | flops | bytes accessed | tf_op | source)
XLA Modules:
  0.0 1136.0 jit_solution(2652462053775522314)
XLA Ops:
  7.2 0.8 add_select_fusion
  8.0 0.7 broadcast_compare_fusion
  9.1 0.8 copy_bitcast_fusion.2
  9.9 1.0 gather_fusion
  10.8 2.7 copy.60
  13.6 2.7 gather.11
  16.7 2.5 copy.61
  19.3 13.1 %all-to-all-start = ((bf16[64,64,256]{2,0,1:T(8,128)(2,1)}), bf16[64,64,256]{2,0,1:T(8,128)(2,1)S(1)}, u32[]{:S(2)}, u32[]{:S(2)}) async-start(bf16[64,64,256]{2,0,1:T(8,128)(2,1)} %copy.61), calls=%async_computation | async-start | bytes 4194304 | tf_op jit(solution)/shard_map/all_to_all | solution.py:77
  33.0 50.6 %all-to-all-done = bf16[64,64,256]{2,0,1:T(8,128)(2,1)S(1)} async-done(((bf16[64,64,256]{2,0,1:T(8,128)(2,1)}), bf16[64,64,256]{2,0,1:T(8,128)(2,1)S(1)}, u32[]{:S(2)}, u32[]{:S(2)}) %all-to-all-start) | async-done | bytes 2097184 | tf_op jit(solution)/shard_map/all_to_all | solution.py:77
  83.6 2.5 copy.62
  86.2 2.7 reshape.238
  88.8 2.7 copy.63
  91.5 2.2 gather_fusion.1
  94.3 5.2 convolution_bitcast_fusion
  99.5 5.2 reshape.241
  104.7 6.6 copy.65
  111.3 6.0 all-to-all-start.1
  118.0 95.2 %all-to-all-done.1 = f32[64,64,256]{2,0,1:T(8,128)} async-done(((f32[64,64,256]{2,0,1:T(8,128)}), f32[64,64,256]{2,0,1:T(8,128)}, u32[]{:S(2)}, u32[]{:S(2)}) %all-to-all-start.1) | async-done | bytes 4194336 | tf_op jit(solution)/shard_map/all_to_all | solution.py:92
  213.2 6.6 copy.66
  219.8 4.7 reshape.242
  224.5 3.6 fusion.30
  228.1 10.8 all_gather.9
  239.0 1.3 convolution_multiply_fusion
  240.3 98.6 %all-gather.3.cloned.1.call-done = f32[16384,256]{1,0:T(8,128)} async-done(((f32[256,256]{1,0:T(8,128)}), f32[16384,256]{1,0:T(8,128)}) %all-gather.3.cloned.1.call-update) | async-done | bytes 16777232 | tf_op jit(solution)/shard_map/all_gather | solution.py:109
  338.9 6.8 reduce_sum.29
  345.8 387.9 %while.36 = (s32[]{:T(128)}, f32[256,256]{1,0:T(8,128)S(1)}, f32[256,256]{1,0:T(8,128)S(1)}, s32[]{:T(128)}, s32[]{:T(128)}, /*index=5*/s32[]{:T(128)}) while((s32[]{:T(128)}, f32[256,256]{1,0:T(8,128)S(1)}, f32[256,256]{1,0:T(8,128)S(1)}, s32[]{:T(128)}, s32[]{:T(128)}, /*index=5*/s32[]{:T(128)}) %tuple.87), condition=%wide.region_5.6_spmd.clone, body=%wide.region_4.5_spmd.clone.sunk | while | flops 132355 | bytes 534141 | solution.py:29
  733.7 394.2 %while.37 = (s32[]{:T(128)}, f32[256,256]{1,0:T(8,128)S(1)}, f32[256,256]{1,0:T(8,128)S(1)}, s32[]{:T(128)}, s32[]{:T(128)}, /*index=5*/s32[]{:T(128)}, s32[]{:T(128)}) while((s32[]{:T(128)}, f32[256,256]{1,0:T(8,128)S(1)}, f32[256,256]{1,0:T(8,128)S(1)}, s32[]{:T(128)}, s32[]{:T(128)}, /*index=5*/s32[]{:T(128)}, s32[]{:T(128)}) %tuple.90), condition=%wide.region_7.8_spmd.clone, body=%wide.region_6.7_spmd.clone.sunk | while | flops 787463 | bytes 268455 | solution.py:46
  734.6 0.6 fusion.52
  736.1 0.6 fusion.52
  737.7 0.6 fusion.52
  739.2 0.6 fusion.52
  740.7 0.6 fusion.52
  742.3 0.6 fusion.52
  743.8 0.6 fusion.52
  745.4 0.6 fusion.52
  746.9 0.6 fusion.52
  748.4 0.6 fusion.52
  750.0 0.6 fusion.52
  751.5 0.6 fusion.52
  753.1 0.6 fusion.52
  754.6 0.6 fusion.52
  756.1 0.6 fusion.52
  757.7 0.6 fusion.52
  759.2 0.6 fusion.52
  760.8 0.6 fusion.52
  762.3 0.6 fusion.52
  763.8 0.6 fusion.52
  1128.0 1.1 fusion.15
  (2578 shorter events, 571.7 us)
Async XLA Ops:
  7.2 86.5 %copy-start = (bf16[1,768,768]{2,1,0:T(8,128)(2,1)S(1)}, bf16[1,768,768]{2,1,0:T(8,128)(2,1)}, u32[]{:S(2)}) copy-start(bf16[1,768,768]{2,1,0:T(8,128)(2,1)} %param.8) | copy-start | bytes 3538948
  19.3 13.1 %copy-start.3 = (s32[64,6]{0,1:T(8,128)S(1)}, s32[64,6]{0,1:T(8,128)}, u32[]{:S(2)}) copy-start(s32[64,6]{0,1:T(8,128)} %param.11) | copy-start | bytes 4612
  19.3 64.4 %all-to-all-start = ((bf16[64,64,256]{2,0,1:T(8,128)(2,1)}), bf16[64,64,256]{2,0,1:T(8,128)(2,1)S(1)}, u32[]{:S(2)}, u32[]{:S(2)}) async-start(bf16[64,64,256]{2,0,1:T(8,128)(2,1)} %copy.61), calls=%async_computation | async-start | bytes 4194304 | tf_op jit(solution)/shard_map/all_to_all | solution.py:77
  111.3 101.9 %all-to-all-start.1 = ((f32[64,64,256]{2,0,1:T(8,128)}), f32[64,64,256]{2,0,1:T(8,128)}, u32[]{:S(2)}, u32[]{:S(2)}) async-start(f32[64,64,256]{2,0,1:T(8,128)} %copy.65), calls=%async_computation.1 | async-start | bytes 8388608 | tf_op jit(solution)/shard_map/all_to_all | solution.py:92
  117.3 221.7 %all-gather.3.cloned.1.call-start = ((), (), s32[]{:S(2)}) async-start(), calls=%async_computation.2 | async-start | bytes 17039360 | tf_op jit(solution)/shard_map/all_gather | solution.py:109
  228.1 117.7 %copy-start.1 = (f32[8,8,3,128]{3,1,2,0:T(8,128)}, f32[8,8,3,128]{3,1,2,0:T(8,128)S(1)}, u32[]{:S(2)}) copy-start(f32[8,8,3,128]{3,1,2,0:T(8,128)S(1)} %copy.79) | copy-start | bytes 294916
  1128.0 1.1 copy-start.2
Sparse Core Ops, SparseCore 0:
  240.4 98.4 all-gather.2
